TPU v7x, 32 devices: a whole 2x2x4 slice. The times are simulated.
32 devices in a mesh: pipe: 4 (over x, core), expert: 8 (over z, y).
Axes of the slice: x: 2, y: 2, z: 4, core: 2. Of those that a mesh axis runs over, the one named last changes fastest.
Arguments:
- activations: bfloat16 [4, 2, 512, 7168], P('pipe', None, 'expert'), may hold values from -6 to 6
- expert_ids: int32 [4, 2, 512], P('pipe', None, 'expert'), may hold values from 0 to 1, as said below
- gate_values: float32 [4, 2, 512], P('pipe', None, 'expert'), may hold values from 0.5 to 1.5
- norm_gain: bfloat16 [4, 7168], P('pipe'), may hold values from 0.25 to 1.75
- up_weight: bfloat16 [4, 7168, 2048], P('pipe', None, 'expert'), may hold values from -0.0625 to 0.0625
- down_weight: bfloat16 [4, 2048, 7168], P('pipe', 'expert'), may hold values from -0.1875 to 0.1875
Outputs:
- received: bfloat16 [4, 2, 512, 7168], P('pipe', None, 'expert')
Inputs may be any that keep to these rules, and one draw needn't show every extreme that they name: `expert_ids`: the 64 tokens of one device in one section and micro-batch (aligned blocks along the last dimension) name no expert more than 48 times; in every section and micro-batch one expert is named exactly 48 times by the tokens of every device.
All inputs are finite; a program needn't handle non-finite values.
Results may differ from a plain program's by a relative error of at most 0.0058.
Values may be sent and summed in bfloat16 or wider, within the bound.
A program may use at most 128 MiB of HBM per device.

v0:
```python
import jax
import jax.numpy as jnp
from jax import lax
from jax.sharding import PartitionSpec as P

LEVELS = 2


EPSILON = 1e-06


def from_behind(value, axis, steps):
    count = lax.axis_size(axis)
    pairs = [(source, (source + steps) % count) for source in range(count)]
    return lax.ppermute(value, axis, pairs)


def expert_rows(arriving, up_local, down_local):
    flattened = arriving.reshape(-1, arriving.shape[-1])
    hidden = jax.nn.silu(jnp.dot(flattened, up_local, preferred_element_type=jnp.float32)).astype(
        jnp.bfloat16
    )
    partial_value = jnp.dot(hidden, down_local, preferred_element_type=jnp.float32).astype(
        jnp.bfloat16
    )
    return partial_value.reshape(arriving.shape[0], arriving.shape[1], down_local.shape[1])


def one_batch(activations, expert_ids, gate_values, norm_gain, up_local, down_local):
    devices = lax.axis_size("expert")
    group_size = 2**LEVELS
    half_group = group_size // 2
    experts_count = devices // group_size
    tok_count = activations.shape[0]
    model_width = activations.shape[1]
    capacity = max(2, 3 * tok_count // (2 * experts_count))
    widened = activations.astype(jnp.float32)
    scale_inv = lax.rsqrt(jnp.mean(widened * widened, axis=-1, keepdims=True) + EPSILON)
    normed = (widened * scale_inv * norm_gain.astype(jnp.float32)).astype(jnp.bfloat16)
    onehot = (expert_ids[:, None] == jnp.arange(experts_count, dtype=jnp.int32)[None, :]).astype(
        jnp.int32
    )
    ranking = jnp.sum((jnp.cumsum(onehot, axis=0) - onehot) * onehot, axis=-1)
    outgoing = (
        jnp.zeros((experts_count, capacity, model_width), jnp.bfloat16)
        .at[expert_ids, ranking]
        .set(normed)
    )
    copies = jnp.repeat(outgoing, group_size, axis=0)
    returned = lax.all_to_all(
        expert_rows(
            lax.all_to_all(copies, "expert", split_axis=0, concat_axis=0, tiled=True),
            up_local,
            down_local,
        ),
        "expert",
        split_axis=0,
        concat_axis=0,
        tiled=True,
    )
    parts_wide = returned.reshape(experts_count, group_size, capacity, model_width).astype(
        jnp.float32
    )
    pairs = (parts_wide[:, :half_group] + parts_wide[:, half_group:]).astype(jnp.bfloat16)
    pairs = lax.optimization_barrier(pairs)
    expert_out = jnp.sum(pairs.astype(jnp.float32), axis=1).astype(jnp.bfloat16)
    gathered = expert_out[expert_ids, ranking]
    return (widened + gate_values[:, None] * gathered.astype(jnp.float32)).astype(jnp.bfloat16)


def local(activations, expert_ids, gate_values, norm_gain, up_weight, down_weight):
    batches = activations.shape[1]
    finished = jnp.stack(
        [
            one_batch(
                activations[0, batch_index],
                expert_ids[0, batch_index],
                gate_values[0, batch_index],
                norm_gain[0],
                up_weight[0],
                down_weight[0],
            )
            for batch_index in range(batches)
        ]
    )
    received = from_behind(finished, "pipe", 1)
    return received[None]


def solution(mesh):
    placed = (
        P("pipe", None, "expert", None),
        P("pipe", None, "expert"),
        P("pipe", None, "expert"),
        P("pipe", None),
        P("pipe", None, "expert"),
        P("pipe", "expert", None),
    )
    return jax.shard_map(
        local,
        mesh=mesh,
        in_specs=placed,
        out_specs=P("pipe", None, "expert", None),
        check_vma=False,
    )
```

profile of v0, /device:TPU:29, one launch (start us, length us, event | category | flops | bytes accessed | tf_op | source)
XLA Modules:
  0.0 577.9 jit_solution(18441530619944495216)
XLA Ops:
  0.0 0.0 copy-start
  0.0 0.8 slice_bitcast_fusion.3
  0.8 0.1 fusion.27
  0.9 0.1 fusion.26
  1.0 0.1 reduce_window_sum.17
  1.1 0.1 reduce_window_sum.18
  1.2 1.9 fusion.12
  3.1 0.8 mul.109
  3.9 0.2 select_reduce_fusion
  4.1 0.8 fusion.30
  4.9 0.0 copy-done
  4.9 1.8 fusion.14
  6.6 0.1 broadcast.133.clone.1
  6.7 19.3 %scatter_fusion.1 = bf16[2,48,7168]{2,1,0:T(8,128)(2,1)S(1)} fusion(bf16[2,48,7168]{2,1,0:T(8,128)(2,1)S(1)} %broadcast.133.clone.1, s32[64]{0:T(128)S(1)} %get-tuple-element.17, bf16[64,7168]{1,0:T(8,128)(2,1)} %get-tuple-element.12), kind=kCustom, calls=%fused_computation.3 | custom fusion | bytes 2753024 | tf_op jit(solution)/shard_map/scatter | solution.py:47
  26.1 3.0 broadcast_in_dim.7
  29.1 5.4 all-to-all-start.2
  34.6 0.1 broadcast.133.clone
  34.7 19.3 %scatter_fusion = bf16[2,48,7168]{2,1,0:T(8,128)(2,1)S(1)} fusion(bf16[2,48,7168]{2,1,0:T(8,128)(2,1)S(1)} %broadcast.133.clone, s32[64]{0:T(128)S(1)} %get-tuple-element.7, bf16[64,7168]{1,0:T(8,128)(2,1)} %get-tuple-element.11), kind=kCustom, calls=%fused_computation.2 | custom fusion | bytes 2753024 | tf_op jit(solution)/shard_map/scatter | solution.py:47
  54.0 100.3 %all-to-all-done.2 = bf16[8,48,7168]{2,1,0:T(8,128)(2,1)} async-done(((bf16[8,48,7168]{2,1,0:T(8,128)(2,1)}), bf16[8,48,7168]{2,1,0:T(8,128)(2,1)}, u32[]{:S(2)}, u32[]{:S(2)}) %all-to-all-start.2) | async-done | bytes 5505056 | tf_op jit(solution)/shard_map/all_to_all | solution.py:52
  154.3 3.0 broadcast_in_dim.6
  157.4 5.4 all-to-all-start
  162.8 0.0 copy-start.1
  162.8 5.4 multiply_convert_fusion
  168.2 0.0 copy-done.1
  168.2 4.0 convolution_convert_fusion
  172.2 110.4 %all-to-all-done = bf16[8,48,7168]{2,1,0:T(8,128)(2,1)} async-done(((bf16[8,48,7168]{2,1,0:T(8,128)(2,1)}), bf16[8,48,7168]{2,1,0:T(8,128)(2,1)}, u32[]{:S(2)}, u32[]{:S(2)}) %all-to-all-start) | async-done | bytes 5505056 | tf_op jit(solution)/shard_map/all_to_all | solution.py:52
  282.6 5.4 all-to-all-start.3
  288.0 0.0 copy-start.2
  288.0 5.4 multiply_convert_fusion.1
  293.4 0.0 copy-done.2
  293.4 4.0 convolution_convert_fusion.1
  297.4 110.2 %all-to-all-done.3 = bf16[8,48,7168]{2,1,0:T(8,128)(2,1)} async-done(((bf16[8,48,7168]{2,1,0:T(8,128)(2,1)}), bf16[8,48,7168]{2,1,0:T(8,128)(2,1)}, u32[]{:S(2)}, u32[]{:S(2)}) %all-to-all-start.3) | async-done | bytes 5505056 | tf_op jit(solution)/shard_map/all_to_all | solution.py:50
  407.6 0.0 copy-start.3
  407.6 5.7 all-to-all-start.1
  413.3 0.0 copy-done.3
  413.3 3.9 convert.12
  417.2 2.2 fusion
  419.4 113.7 %all-to-all-done.1 = bf16[8,48,7168]{2,1,0:T(8,128)(2,1)} async-done(((bf16[8,48,7168]{2,1,0:T(8,128)(2,1)}), bf16[8,48,7168]{2,1,0:T(8,128)(2,1)}, u32[]{:S(2)}, u32[]{:S(2)}) %all-to-all-start.1) | async-done | bytes 5505056 | tf_op jit(solution)/shard_map/all_to_all | solution.py:50
  533.1 3.9 convert.11
  537.0 2.2 fusion.1
  539.2 2.4 reduce_sum.71
  541.6 4.3 gather_fusion.1
  545.9 2.4 reduce_sum.67
  548.3 4.2 gather_fusion
  552.5 2.1 fusion.16
  554.7 0.2 pad_maximum_fusion
  554.8 1.6 collective-permute-start
  556.5 20.2 %collective-permute-done = bf16[2,64,7168]{2,1,0:T(8,128)(2,1)S(1)} collective-permute-done((bf16[2,64,7168]{2,1,0:T(8,128)(2,1)S(1)}, bf16[2,64,7168]{2,1,0:T(8,128)(2,1)S(1)}, u32[]{:S(2)}, u32[]{:S(2)}) %collective-permute-start) | collective-permute-done | bytes 1835040 | tf_op jit(solution)/shard_map/ppermute | solution.py:15
  576.6 1.2 copy.12
  (2 shorter events, 0.0 us)
Async XLA Ops:
  0.0 4.9 copy-start
  29.1 125.2 %all-to-all-start.2 = ((bf16[8,48,7168]{2,1,0:T(8,128)(2,1)}), bf16[8,48,7168]{2,1,0:T(8,128)(2,1)}, u32[]{:S(2)}, u32[]{:S(2)}) async-start(bf16[8,48,7168]{2,1,0:T(8,128)(2,1)} %bitcast.116), calls=%async_computation.2 | async-start | bytes 11010048 | tf_op jit(solution)/shard_map/all_to_all | solution.py:52
  157.4 125.2 %all-to-all-start = ((bf16[8,48,7168]{2,1,0:T(8,128)(2,1)}), bf16[8,48,7168]{2,1,0:T(8,128)(2,1)}, u32[]{:S(2)}, u32[]{:S(2)}) async-start(bf16[8,48,7168]{2,1,0:T(8,128)(2,1)} %bitcast.117), calls=%async_computation | async-start | bytes 11010048 | tf_op jit(solution)/shard_map/all_to_all | solution.py:52
  162.8 5.4 copy-start.1
  282.6 125.1 %all-to-all-start.3 = ((bf16[8,48,7168]{2,1,0:T(8,128)(2,1)}), bf16[8,48,7168]{2,1,0:T(8,128)(2,1)}, u32[]{:S(2)}, u32[]{:S(2)}) async-start(bf16[8,48,7168]{2,1,0:T(8,128)(2,1)} %bitcast.115), calls=%async_computation.3 | async-start | bytes 11010048 | tf_op jit(solution)/shard_map/all_to_all | solution.py:50
  288.0 5.4 copy-start.2
  407.6 5.7 copy-start.3
  407.6 125.5 %all-to-all-start.1 = ((bf16[8,48,7168]{2,1,0:T(8,128)(2,1)}), bf16[8,48,7168]{2,1,0:T(8,128)(2,1)}, u32[]{:S(2)}, u32[]{:S(2)}) async-start(bf16[8,48,7168]{2,1,0:T(8,128)(2,1)} %bitcast.114), calls=%async_computation.1 | async-start | bytes 11010048 | tf_op jit(solution)/shard_map/all_to_all | solution.py:50
  554.8 21.8 %collective-permute-start = (bf16[2,64,7168]{2,1,0:T(8,128)(2,1)S(1)}, bf16[2,64,7168]{2,1,0:T(8,128)(2,1)S(1)}, u32[]{:S(2)}, u32[]{:S(2)}) collective-permute-start(bf16[2,64,7168]{2,1,0:T(8,128)(2,1)S(1)} %pad_maximum_fusion), channel_id=1, source_target_pairs={{0,8},{8,16},{16,24},{24,0},{1,9},{9,17},{17,25},{25,1},{2,10},{10... | collective-permute-start | bytes 5505032 | tf_op jit(solution)/shard_map/ppermute | solution.py:15
where the time goes:
time: 583 us; the launch traced here: 578 us
  waiting for transfers between devices  455 us (78%)
  local copies, waits for them, and re-layouts  55.6 us (10%)
  other arithmetic  25 us (4%)
  starting transfers between devices  23.7 us (4%)
  matrix products  18.8 us (3%)
    all_to_all x2, waiting for transfers between devices, one_batch(): lax.all_to_all(expert_rows(lax.all_to_all(copies, 'expert', split_axis=0,...  224 us
    all_to_all x2, waiting for transfers between devices, one_batch(): lax.all_to_all(copies, 'expert', split_axis=0, concat_axis=0, tiled=True)  211 us
    scatter x2, local copies, waits for them, and re-layouts, one_batch(): outgoing = jnp.zeros((experts_count, capacity, model_width), jnp.bfloat16...  38.7 us
    ppermute x1, waiting for transfers between devices, from_behind(): return lax.ppermute(value, axis, pairs)  20.2 us
  transfers between devices with their start and end apart: 5, of which 5 were waited for; matrix products, arithmetic and copies ran while one was open for 8% of the time, Pallas kernels for 0%

commit v1 on v0

v1 whole, which is shorter than its diff:
```python
import jax
import jax.numpy as jnp
from jax import lax
from jax.sharding import PartitionSpec as P

LEVELS = 2


EPSILON = 1e-06


def from_behind(value, axis, steps):
    count = lax.axis_size(axis)
    pairs = [(source, (source + steps) % count) for source in range(count)]
    return lax.ppermute(value, axis, pairs)


def one_batch(activations, expert_ids, gate_values, norm_gain, up_local, down_local):
    group_size = 2**LEVELS
    mine = lax.axis_index("expert") // group_size
    widened = activations.astype(jnp.float32)
    scale_inv = lax.rsqrt(jnp.mean(widened * widened, axis=-1, keepdims=True) + EPSILON)
    normed = (widened * scale_inv * norm_gain.astype(jnp.float32)).astype(jnp.bfloat16)
    every = lax.all_gather(normed, "expert", axis=0, tiled=True)
    ids = lax.all_gather(expert_ids, "expert", axis=0, tiled=True)
    hidden = jax.nn.silu(jnp.dot(every, up_local, preferred_element_type=jnp.float32))
    hidden = jnp.where((ids == mine)[:, None], hidden, 0.0).astype(jnp.bfloat16)
    partial_value = jnp.dot(hidden, down_local, preferred_element_type=jnp.float32).astype(jnp.bfloat16)
    expert_out = lax.psum_scatter(partial_value, "expert", scatter_dimension=0, tiled=True)
    return (widened + gate_values[:, None] * expert_out.astype(jnp.float32)).astype(jnp.bfloat16)


def local(activations, expert_ids, gate_values, norm_gain, up_weight, down_weight):
    batches = activations.shape[1]
    received = [
        from_behind(
            one_batch(
                activations[0, batch_index],
                expert_ids[0, batch_index],
                gate_values[0, batch_index],
                norm_gain[0],
                up_weight[0],
                down_weight[0],
            ),
            "pipe",
            1,
        )
        for batch_index in range(batches)
    ]
    return jnp.stack(received)[None]


def solution(mesh):
    placed = (
        P("pipe", None, "expert", None),
        P("pipe", None, "expert"),
        P("pipe", None, "expert"),
        P("pipe", None),
        P("pipe", None, "expert"),
        P("pipe", "expert", None),
    )
    return jax.shard_map(
        local,
        mesh=mesh,
        in_specs=placed,
        out_specs=P("pipe", None, "expert", None),
        check_vma=False,
    )
```

time: 583 us -> 543 us (0.931)
  local copies, waits for them, and re-layouts: 55.6 us -> 1.52 us
  starting transfers between devices: 23.7 us -> 1.94 us
  waiting for transfers between devices: 455 us -> 474 us
  other arithmetic: 25 us -> 9.52 us
  between operations: 0.14 us -> 13.9 us
  matrix products: 18.8 us -> 31.9 us
    all_to_all x4 -> x0, waiting for transfers between devices: 435 us -> none  [the longest x2 224 us: one_batch(): lax.all_to_all(expert_rows(lax.all_to_all(copies, 'expert', split_axis=0,...]
    reduce_scatter x0 -> x2, waiting for transfers between devices: none -> 254 us  [one_batch(): lax.psum_scatter(partial_value, 'expert', scatter_dimension=0, tiled=True)]
    all_gather x0 -> x2, waiting for transfers between devices: none -> 199 us  [one_batch(): every = lax.all_gather(normed, 'expert', axis=0, tiled=True)]
    scatter x2 -> x0, local copies, waits for them, and re-layouts: 38.7 us -> none  [one_batch(): outgoing = jnp.zeros((experts_count, capacity, model_width), jnp.bfloat16...]
    all_to_all x4 -> x0, starting transfers between devices: 22 us -> none  [the longest x2 11.1 us: one_batch(): lax.all_to_all(expert_rows(lax.all_to_all(copies, 'expert', split_axis=0,...]
    dot_general x4 -> x2, matrix products: 18.8 us -> 31.9 us  [one_batch(): jnp.dot(hidden, down_local, preferred_element_type=jnp.float32)]
    convert_element_type x7 -> x1, other arithmetic: 14.5 us -> 2.14 us  [one_batch(): (widened + gate_values[:, None] * expert_out.astype(jnp.float32)).astype(...]
    gather x2 -> x0, local copies, waits for them, and re-layouts: 8.52 us -> none  [one_batch(): gathered = expert_out[expert_ids, ranking]]
  transfers between devices with their start and end apart: 5 -> 6, of which waited for: 5 -> 6; matrix products, arithmetic and copies ran while one was open for 8% -> 6% of each run, Pallas kernels for 0% -> 0%
where the time goes in v1:
time: 543 us; the launch traced here: 538 us
  waiting for transfers between devices  474 us (87%)
  matrix products  31.9 us (6%)
  between operations  13.9 us (3%)
  other arithmetic  9.52 us (2%)
  blocking collectives  5.61 us (1%)
    reduce_scatter x2, waiting for transfers between devices, one_batch(): lax.psum_scatter(partial_value, 'expert', scatter_dimension=0, tiled=True)  254 us
    all_gather x2, waiting for transfers between devices, one_batch(): every = lax.all_gather(normed, 'expert', axis=0, tiled=True)  199 us
    dot_general x2, matrix products, one_batch(): jnp.dot(hidden, down_local, preferred_element_type=jnp.float32)  31.9 us
    ppermute x2, waiting for transfers between devices, from_behind(): return lax.ppermute(value, axis, pairs)  20.1 us
  transfers between devices with their start and end apart: 6, of which 6 were waited for; matrix products, arithmetic and copies ran while one was open for 6% of the time, Pallas kernels for 0%

profile of v1, /device:TPU:29, one launch (start us, length us, event | category | flops | bytes accessed | tf_op | source)
XLA Modules:
  0.0 538.0 jit_solution(1292191055187865386)
XLA Ops:
  6.5 0.0 copy-start.3
  6.5 0.0 copy-start.2
  6.5 0.0 all-gather.5.cloned.1.call-start
  6.5 1.9 fusion.6
  8.5 0.8 mul.87
  9.3 3.2 fusion.8
  12.5 0.0 all-gather.5.cloned.1.call-update
  12.6 0.0 all-gather.7.cloned.1.call-start
  12.6 0.7 all-gather.7.cloned.1.call-update
  13.3 0.0 reduce-scatter.3.cloned.1.call-start
  13.4 0.0 copy-done.3
  13.4 0.7 dynamic-slice
  14.8 0.0 copy-done.2
  14.8 0.1 bitcast_dynamic-update-slice_fusion
  14.9 0.1 bitcast_dynamic-update-slice_fusion.1
  15.0 5.6 %all-reduce.2 = (s32[512]{0:T(512)S(1)}, s32[512]{0:T(512)S(1)}) all-reduce(s32[512]{0:T(512)S(1)} %bitcast_dynamic-update-slice_fusion, s32[512]{0:T(512)S(1)} %bitcast_dynamic-update-slice_fusion.1), channel_id=3, replica_groups=mesh['pipe'=4,'expert'=8] {'expert'}, use_global_device_ids=true, to_apply=%add.1 | all-reduce | flops 1024 | bytes 8192
  20.6 102.4 %all-gather.5.cloned.1.call-done = bf16[512,7168]{1,0:T(8,128)(2,1)} async-done(((bf16[64,7168]{1,0:T(8,128)(2,1)}), bf16[512,7168]{1,0:T(8,128)(2,1)}) %all-gather.5.cloned.1.call-update) | async-done | bytes 7340048 | tf_op jit(solution)/shard_map/all_gather | solution.py:24
  122.9 15.9 %convolution_convert_fusion.1 = bf16[512,7168]{1,0:T(8,128)(2,1)} fusion(bf16[1,256,7168]{2,1,0:T(8,128)(2,1)} %param.11, bf16[512,7168]{1,0:T(8,128)(2,1)} %all-gather.5.cloned.1.call-done, bf16[1,7168,256]{2,1,0:T(8,128)(2,1)} %param.10, pred[512]{0:T(512)(128)(4,1)S(1)} %broadcast_compare_fusion.1), kind=kOutput, calls=%fused_computation.1 | convolution fusion | flops 3762552832 | bytes 22020608 | tf_op jit(solution)/shard_map/dot_general | solution.py:28
  138.8 0.0 reduce-scatter.3.cloned.1.call-update
  138.9 0.2 reduce-scatter.5.cloned.1.call-start
  139.1 96.2 %all-gather.7.cloned.1.call-done = bf16[512,7168]{1,0:T(8,128)(2,1)} async-done(((bf16[64,7168]{1,0:T(8,128)(2,1)}), bf16[512,7168]{1,0:T(8,128)(2,1)}) %all-gather.7.cloned.1.call-update) | async-done | bytes 7340048 | tf_op jit(solution)/shard_map/all_gather | solution.py:24
  235.3 16.0 %convolution_convert_fusion = bf16[512,7168]{1,0:T(8,128)(2,1)} fusion(bf16[1,256,7168]{2,1,0:T(8,128)(2,1)} %param.11, bf16[512,7168]{1,0:T(8,128)(2,1)} %all-gather.7.cloned.1.call-done, bf16[1,7168,256]{2,1,0:T(8,128)(2,1)} %param.10, pred[512]{0:T(512)(128)(4,1)S(1)} %broadcast_compare_fusion), kind=kOutput, calls=%fused_computation | convolution fusion | flops 3762552832 | bytes 22020608 | tf_op jit(solution)/shard_map/dot_general | solution.py:28
  251.3 0.0 copy-start.1
  251.3 0.0 copy-start
  251.3 0.0 reduce-scatter.5.cloned.1.call-update
  251.4 0.7 copy-done.1
  252.0 118.9 %reduce-scatter.3.cloned.1.call-done = bf16[64,7168]{1,0:T(8,128)(2,1)} async-done(((bf16[512,7168]{1,0:T(8,128)(2,1)}), bf16[64,7168]{1,0:T(8,128)(2,1)}) %reduce-scatter.3.cloned.1.call-update) | async-done | bytes 917520 | tf_op jit(solution)/shard_map/reduce_scatter | solution.py:29
  370.9 135.3 %reduce-scatter.5.cloned.1.call-done = bf16[64,7168]{1,0:T(8,128)(2,1)} async-done(((bf16[512,7168]{1,0:T(8,128)(2,1)}), bf16[64,7168]{1,0:T(8,128)(2,1)}) %reduce-scatter.5.cloned.1.call-update) | async-done | bytes 917520 | tf_op jit(solution)/shard_map/reduce_scatter | solution.py:29
  506.1 0.0 copy-done
  506.2 2.1 fusion.9
  508.3 1.6 collective-permute-start
  509.9 0.1 collective-permute-start.1
  509.9 10.3 %collective-permute-done = bf16[64,7168]{1,0:T(8,128)(2,1)S(1)} collective-permute-done((bf16[64,7168]{1,0:T(8,128)(2,1)S(1)}, bf16[64,7168]{1,0:T(8,128)(2,1)S(1)}, u32[]{:S(2)}, u32[]{:S(2)}) %collective-permute-start) | collective-permute-done | bytes 917536 | tf_op jit(solution)/shard_map/ppermute | solution.py:15
  520.2 9.8 %collective-permute-done.1 = bf16[64,7168]{1,0:T(8,128)(2,1)S(1)} collective-permute-done((bf16[64,7168]{1,0:T(8,128)(2,1)S(1)}, bf16[64,7168]{1,0:T(8,128)(2,1)S(1)}, u32[]{:S(2)}, u32[]{:S(2)}) %collective-permute-start.1) | collective-permute-done | bytes 917536 | tf_op jit(solution)/shard_map/ppermute | solution.py:15
  530.0 1.4 maximum_bitcast_fusion
  (6 shorter events, 0.0 us)
Async XLA Ops:
  6.5 6.8 %copy-start.3 = (u32[32]{0:T(128)S(1)}, u32[32]{0:T(128)}, u32[]{:S(2)}) copy-start(u32[32]{0:T(128)} %constant.42) | copy-start | bytes 388
  6.5 8.2 %copy-start.2 = (s32[1,2,64]{2,1,0:T(2,128)S(1)}, s32[1,2,64]{2,1,0:T(2,128)}, u32[]{:S(2)}) copy-start(s32[1,2,64]{2,1,0:T(2,128)} %param.7) | copy-start | bytes 1540
  6.5 116.4 %all-gather.5.cloned.1.call-start = ((), (), s32[]{:S(2)}) async-start(), calls=%async_computation.2 | async-start | bytes 8257536 | tf_op jit(solution)/shard_map/all_gather | solution.py:24
  12.6 222.8 %all-gather.7.cloned.1.call-start = ((), (), s32[]{:S(2)}) async-start(), calls=%async_computation.4 | async-start | bytes 8257536 | tf_op jit(solution)/shard_map/all_gather | solution.py:24
  13.3 357.6 %reduce-scatter.3.cloned.1.call-start = ((), (), s32[]{:S(2)}) async-start(), calls=%async_computation.3 | async-start | bytes 8257536 | tf_op jit(solution)/shard_map/reduce_scatter | solution.py:29
  138.9 367.3 %reduce-scatter.5.cloned.1.call-start = ((), (), s32[]{:S(2)}) async-start(), calls=%async_computation.5 | async-start | bytes 8257536 | tf_op jit(solution)/shard_map/reduce_scatter | solution.py:29
  251.3 0.7 copy-start.1
  251.3 254.8 %copy-start = (bf16[1,2,64,7168]{3,2,1,0:T(8,128)(2,1)S(1)}, bf16[1,2,64,7168]{3,2,1,0:T(8,128)(2,1)}, u32[]{:S(2)}) copy-start(bf16[1,2,64,7168]{3,2,1,0:T(8,128)(2,1)} %param.6) | copy-start | bytes 5505028
  508.3 11.9 %collective-permute-start = (bf16[64,7168]{1,0:T(8,128)(2,1)S(1)}, bf16[64,7168]{1,0:T(8,128)(2,1)S(1)}, u32[]{:S(2)}, u32[]{:S(2)}) collective-permute-start(bf16[64,7168]{1,0:T(8,128)(2,1)S(1)} %get-tuple-element.11), channel_id=1, source_target_pairs={{0,8},{8,16},{16,24},{24,0},{1,9},{9,17},{17,25},{25,1},{2,10},{10... | collective-permute-start | bytes 2752520 | tf_op jit(solution)/shard_map/ppermute | solution.py:15
  509.9 20.2 %collective-permute-start.1 = (bf16[64,7168]{1,0:T(8,128)(2,1)S(1)}, bf16[64,7168]{1,0:T(8,128)(2,1)S(1)}, u32[]{:S(2)}, u32[]{:S(2)}) collective-permute-start(bf16[64,7168]{1,0:T(8,128)(2,1)S(1)} %get-tuple-element.12), channel_id=1, source_target_pairs={{0,8},{8,16},{16,24},{24,0},{1,9},{9,17},{17,25},{25,1},{2,10},{10... | collective-permute-start | bytes 2752520 | tf_op jit(solution)/shard_map/ppermute | solution.py:15
Sparse Core Ops, SparseCore 0:
  12.7 110.2 all-gather.4
  125.1 110.1 all-gather.6
  238.9 131.9 reduce-scatter.2
  374.3 131.7 reduce-scatter.4

commit v2 on v1

v2 whole, which is shorter than its diff:
```python
import jax
import jax.numpy as jnp
from jax import lax
from jax.sharding import PartitionSpec as P

LEVELS = 2


EPSILON = 1e-06


def from_behind(value, axis, steps):
    count = lax.axis_size(axis)
    pairs = [(source, (source + steps) % count) for source in range(count)]
    return lax.ppermute(value, axis, pairs)


def exchange(value, groups=None):
    return lax.all_to_all(
        value, "expert", split_axis=0, concat_axis=0, tiled=True, axis_index_groups=groups
    )


def local(activations, expert_ids, gate_values, norm_gain, up_weight, down_weight):
    devices = lax.axis_size("expert")
    group = 2**LEVELS
    experts = devices // group
    groups = [[e * group + j for j in range(group)] for e in range(experts)]
    _, batches, tok, width = activations.shape
    part = width // group
    units = up_weight.shape[2]
    capacity = max(2, 3 * tok // (2 * experts))
    f32, bf16 = jnp.float32, jnp.bfloat16

    up_part = exchange(up_weight[0].reshape(group, part, units), groups)
    down_part = exchange(down_weight[0].reshape(units, group, part).transpose(1, 0, 2), groups)
    down_part = down_part.reshape(group * units, part)

    widened = activations[0].astype(f32)
    scale_inv = lax.rsqrt(jnp.mean(widened * widened, axis=-1, keepdims=True) + EPSILON)
    normed = (widened * scale_inv * norm_gain[0].astype(f32)).astype(bf16)
    onehot = (expert_ids[0][..., None] == jnp.arange(experts, dtype=jnp.int32)).astype(jnp.int32)
    ranking = jnp.sum((jnp.cumsum(onehot, axis=1) - onehot) * onehot, axis=-1)
    slot = expert_ids[0] * capacity + ranking
    place = (slot[..., None] == jnp.arange(experts * capacity, dtype=jnp.int32)).astype(bf16)

    pres = []
    for m in range(batches):
        packed = lax.dot_general(
            place[m], normed[m], (((0,), (0,)), ((), ())), preferred_element_type=f32
        ).astype(bf16)
        packed = packed.reshape(experts, capacity, group, part).transpose(0, 2, 1, 3)
        arriving = exchange(packed.reshape(devices, capacity, part)).reshape(-1, part)
        pres.append(
            jnp.stack([jnp.dot(arriving, up_part[j], preferred_element_type=f32).astype(bf16) for j in range(group)])
        )
    summed = exchange(jnp.concatenate(pres, axis=1), groups).astype(f32)
    hidden = jax.nn.silu(jnp.sum(summed, axis=0)).astype(bf16)
    hidden = exchange(jnp.broadcast_to(hidden[None], (group,) + hidden.shape), groups)
    rows = devices * capacity
    received = []
    for m in range(batches):
        mine = hidden[:, m * rows : (m + 1) * rows]
        mine = jnp.concatenate([mine[j] for j in range(group)], axis=1)
        out = jnp.dot(mine, down_part, preferred_element_type=f32).astype(bf16)
        returned = exchange(out.reshape(devices, capacity, part))
        returned = returned.reshape(experts, group, capacity, part).transpose(0, 2, 1, 3)
        expert_out = jnp.dot(
            place[m], returned.reshape(experts * capacity, width), preferred_element_type=f32
        )
        layer_out = (widened[m] + gate_values[0, m][:, None] * expert_out).astype(bf16)
        received.append(from_behind(layer_out, "pipe", 1))
    return jnp.stack(received)[None]


def solution(mesh):
    placed = (
        P("pipe", None, "expert", None),
        P("pipe", None, "expert"),
        P("pipe", None, "expert"),
        P("pipe", None),
        P("pipe", None, "expert"),
        P("pipe", "expert", None),
    )
    return jax.shard_map(
        local,
        mesh=mesh,
        in_specs=placed,
        out_specs=P("pipe", None, "expert", None),
        check_vma=False,
    )
```

time: 543 us -> 335 us (0.62)
  waiting for transfers between devices: 474 us -> 183 us
  starting transfers between devices: 1.94 us -> 40.5 us
  blocking collectives: 5.61 us -> 36.1 us
  local copies, waits for them, and re-layouts: 1.52 us -> 27.4 us
  between operations: 13.9 us -> 0.21 us
    reduce_scatter x2 -> x0, waiting for transfers between devices: 254 us -> none  [one_batch(): lax.psum_scatter(partial_value, 'expert', scatter_dimension=0, tiled=True)]
    all_gather x2 -> x0, waiting for transfers between devices: 199 us -> none  [one_batch(): every = lax.all_gather(normed, 'expert', axis=0, tiled=True)]
    all_to_all x0 -> x7, waiting for transfers between devices: none -> 172 us  [exchange(): lax.all_to_all(value, 'expert', split_axis=0, concat_axis=0, tiled=True,...]
    all_to_all x0 -> x1, blocking collectives: none -> 36.1 us  [exchange(): lax.all_to_all(value, 'expert', split_axis=0, concat_axis=0, tiled=True,...]
    all_to_all x0 -> x7, starting transfers between devices: none -> 35.8 us  [exchange(): lax.all_to_all(value, 'expert', split_axis=0, concat_axis=0, tiled=True,...]
    ppermute x2, waiting for transfers between devices: 20.1 us -> 10.3 us  [from_behind(): return lax.ppermute(value, axis, pairs)]
    reshape x0 -> x4, local copies, waits for them, and re-layouts: none -> 7.59 us  [local(): packed.reshape(experts, capacity, group, part).transpose(0, 2, 1, 3)]
    unnamed x13 -> x23, local copies, waits for them, and re-layouts: 1.52 us -> 8.79 us
  transfers between devices with their start and end apart: 6 -> 9, of which waited for: 6 -> 8; matrix products, arithmetic and copies ran while one was open for 6% -> 12% of each run, Pallas kernels for 0% -> 0%
where the time goes in v2:
time: 335 us; the launch traced here: 328 us
  waiting for transfers between devices  183 us (55%)
  starting transfers between devices  40.5 us (12%)
  blocking collectives  36.1 us (11%)
  matrix products  32.4 us (10%)
  local copies, waits for them, and re-layouts  27.4 us (8%)
  other arithmetic  9.38 us (3%)
    all_to_all x7, waiting for transfers between devices, exchange(): lax.all_to_all(value, 'expert', split_axis=0, concat_axis=0, tiled=True,...  172 us
    all_to_all x1, blocking collectives, exchange(): lax.all_to_all(value, 'expert', split_axis=0, concat_axis=0, tiled=True,...  36.1 us
    all_to_all x7, starting transfers between devices, exchange(): lax.all_to_all(value, 'expert', split_axis=0, concat_axis=0, tiled=True,...  35.8 us
    dot_general x8, matrix products, local(): jnp.dot(arriving, up_part[j], preferred_element_type=f32).astype(bf16)  17.4 us
    ppermute x2, waiting for transfers between devices, from_behind(): return lax.ppermute(value, axis, pairs)  10.3 us
    dot_general x2, matrix products, local(): out = jnp.dot(mine, down_part, preferred_element_type=f32).astype(bf16)  9.73 us
    unnamed x23, local copies, waits for them, and re-layouts  8.79 us
    reshape x4, local copies, waits for them, and re-layouts, local(): packed.reshape(experts, capacity, group, part).transpose(0, 2, 1, 3)  7.59 us
  transfers between devices with their start and end apart: 9, of which 8 were waited for; matrix products, arithmetic and copies ran while one was open for 12% of the time, Pallas kernels for 0%

profile of v2, /device:TPU:29, one launch (start us, length us, event | category | flops | bytes accessed | tf_op | source)
XLA Modules:
  0.0 328.5 jit_solution(16912426260444826749)
XLA Ops:
  0.0 0.9 fusion.29
  0.9 0.1 reduce_window_sum.11
  1.0 0.9 select_reduce_fusion
  1.9 0.7 multiply_add_fusion
  2.6 0.1 iota_compare_fusion
  2.6 0.8 convert_element_type.97
  3.4 2.0 fusion.4
  5.4 0.5 fusion.6
  5.9 0.0 copy-start.3
  5.9 1.2 copy-done.3
  7.2 1.7 convolution_convert_fusion
  8.8 2.9 reshape.81
  11.8 0.1 copy.10
  11.9 36.1 %all_to_all.40 = bf16[8,48,1792]{2,1,0:T(8,128)(2,1)} all-to-all(bf16[8,48,1792]{2,1,0:T(8,128)(2,1)S(1)} %bitcast.133), channel_id=1, replica_groups=mesh['pipe'=4,'expert'=8] {'expert'}, dimensions={0} | all-to-all | bytes 2752512 | tf_op jit(solution)/shard_map/all_to_all | solution.py:19
  48.0 5.4 %all-to-all-start.1 = ((bf16[4,1792,256]{2,1,0:T(8,128)(2,1)}), bf16[4,1792,256]{2,1,0:T(8,128)(2,1)}, u32[]{:S(2)}, u32[]{:S(2)}) async-start(bf16[4,1792,256]{2,1,0:T(8,128)(2,1)} %bitcast.136), calls=%async_computation.1 | async-start | bytes 7340032 | tf_op jit(solution)/shard_map/all_to_all | solution.py:19
  53.4 1.7 convolution_convert_fusion.1
  55.2 1.9 reshape.78
  57.1 2.6 copy.9
  59.7 34.6 %all-to-all-done.1 = bf16[4,1792,256]{2,1,0:T(8,128)(2,1)} async-done(((bf16[4,1792,256]{2,1,0:T(8,128)(2,1)}), bf16[4,1792,256]{2,1,0:T(8,128)(2,1)}, u32[]{:S(2)}, u32[]{:S(2)}) %all-to-all-start.1) | async-done | bytes 3670048 | tf_op jit(solution)/shard_map/all_to_all | solution.py:19
  94.3 5.7 %all-to-all-start = ((bf16[8,48,1792]{2,1,0:T(8,128)(2,1)}), bf16[8,48,1792]{2,1,0:T(8,128)(2,1)}, u32[]{:S(2)}, u32[]{:S(2)}) async-start(bf16[8,48,1792]{2,1,0:T(8,128)(2,1)} %bitcast.8), calls=%async_computation | async-start | bytes 2752512 | tf_op jit(solution)/shard_map/all_to_all | solution.py:19
  100.0 1.7 fusion.11
  101.7 2.4 fusion.12
  104.1 2.4 fusion.13
  106.5 2.4 fusion.14
  108.9 22.3 %all-to-all-done = bf16[8,48,1792]{2,1,0:T(8,128)(2,1)} async-done(((bf16[8,48,1792]{2,1,0:T(8,128)(2,1)}), bf16[8,48,1792]{2,1,0:T(8,128)(2,1)}, u32[]{:S(2)}, u32[]{:S(2)}) %all-to-all-start) | async-done | bytes 1376288 | tf_op jit(solution)/shard_map/all_to_all | solution.py:19
  131.2 2.1 fusion.10
  133.3 2.1 fusion.7
  135.4 2.1 fusion.8
  137.6 0.0 copy-start.8
  137.6 2.2 fusion.9
  139.8 1.3 maximum_maximum_fusion
  141.1 3.6 %all-to-all-start.3 = ((bf16[4,768,256]{2,1,0:T(8,128)(2,1)}), bf16[4,768,256]{2,1,0:T(8,128)(2,1)S(1)}, u32[]{:S(2)}, u32[]{:S(2)}) async-start(bf16[4,768,256]{2,1,0:T(8,128)(2,1)} %maximum_maximum_fusion), calls=%async_computation.3 | async-start | bytes 3145728 | tf_op jit(solution)/shard_map/all_to_all | solution.py:19
  144.7 5.9 %copy.11 = bf16[1,256,7168]{1,2,0:T(8,128)(2,1)} copy(bf16[1,256,7168]{2,1,0:T(8,128)(2,1)} %param.11) | data formatting | bytes 7340032 | tf_op args[5]
  150.7 12.3 %all-to-all-done.3 = bf16[4,768,256]{2,1,0:T(8,128)(2,1)S(1)} async-done(((bf16[4,768,256]{2,1,0:T(8,128)(2,1)}), bf16[4,768,256]{2,1,0:T(8,128)(2,1)S(1)}, u32[]{:S(2)}, u32[]{:S(2)}) %all-to-all-start.3) | async-done | bytes 1572896 | tf_op jit(solution)/shard_map/all_to_all | solution.py:19
  163.0 5.3 %all-to-all-start.5 = ((bf16[4,256,1792]{1,2,0:T(8,128)(2,1)}), bf16[4,256,1792]{1,2,0:T(8,128)(2,1)}, u32[]{:S(2)}, u32[]{:S(2)}) async-start(bf16[4,256,1792]{1,2,0:T(8,128)(2,1)} %bitcast.129), calls=%async_computation.5 | async-start | bytes 7340032 | tf_op jit(solution)/shard_map/all_to_all | solution.py:19
  168.2 0.2 convert_reduce_fusion
  168.4 0.2 multiply_convert_fusion
  168.7 40.4 %all-to-all-done.5 = bf16[4,256,1792]{1,2,0:T(8,128)(2,1)} async-done(((bf16[4,256,1792]{1,2,0:T(8,128)(2,1)}), bf16[4,256,1792]{1,2,0:T(8,128)(2,1)}, u32[]{:S(2)}, u32[]{:S(2)}) %all-to-all-start.5) | async-done | bytes 3670048 | tf_op jit(solution)/shard_map/all_to_all | solution.py:19
  209.0 1.2 broadcast_in_dim.4
  210.3 4.5 %all-to-all-start.4 = ((bf16[4,768,256]{2,1,0:T(8,128)(2,1)}), bf16[4,768,256]{2,1,0:T(8,128)(2,1)S(1)}, u32[]{:S(2)}, u32[]{:S(2)}) async-start(bf16[4,768,256]{2,1,0:T(8,128)(2,1)} %broadcast_in_dim.4), calls=%async_computation.4 | async-start | bytes 3145728 | tf_op jit(solution)/shard_map/all_to_all | solution.py:19
  214.7 5.9 %copy.12 = bf16[4,256,1792]{2,1,0:T(8,128)(2,1)} copy(bf16[4,256,1792]{1,2,0:T(8,128)(2,1)} %all-to-all-done.5) | data formatting | bytes 7340032 | tf_op jit(solution)/shard_map/all_to_all | solution.py:19
  220.7 12.3 %all-to-all-done.4 = bf16[4,768,256]{2,1,0:T(8,128)(2,1)S(1)} async-done(((bf16[4,768,256]{2,1,0:T(8,128)(2,1)}), bf16[4,768,256]{2,1,0:T(8,128)(2,1)S(1)}, u32[]{:S(2)}, u32[]{:S(2)}) %all-to-all-start.4) | async-done | bytes 1572896 | tf_op jit(solution)/shard_map/all_to_all | solution.py:19
  233.0 0.9 slice_bitcast_fusion.25
  233.9 4.7 %convolution_convert_fusion.3 = bf16[384,1792]{1,0:T(8,128)(2,1)} fusion(bf16[1024,1792]{1,0:T(8,128)(2,1)} %bitcast.137, bf16[384,256]{1,0:T(8,128)(2,1)S(1)} %get-tuple-element.10, bf16[384,256]{1,0:T(8,128)(2,1)S(1)} %get-tuple-element.11, bf16[384,256]{1,0:T(8,128)(2,1)S(1)} %get-tuple-element.12, bf16[384,256]{1,0:T(8,128)(2,1)S(1)} %get-tuple-element.5), kind=kOutput, calls=%fused_computation.15 | convolution fusion | flops 1413120000 | bytes 5832704 | tf_op jit(solution)/shard_map/dot_general | solution.py:65
  238.6 5.8 %all-to-all-start.6 = ((bf16[8,48,1792]{2,1,0:T(8,128)(2,1)}), bf16[8,48,1792]{2,1,0:T(8,128)(2,1)S(1)}, u32[]{:S(2)}, u32[]{:S(2)}) async-start(bf16[8,48,1792]{2,1,0:T(8,128)(2,1)} %bitcast.144), calls=%async_computation.6 | async-start | bytes 2752512 | tf_op jit(solution)/shard_map/all_to_all | solution.py:19
  244.5 5.0 %convolution_convert_fusion.2 = bf16[384,1792]{1,0:T(8,128)(2,1)} fusion(bf16[1024,1792]{1,0:T(8,128)(2,1)} %bitcast.138, bf16[384,256]{1,0:T(8,128)(2,1)S(1)} %copy-done.5, bf16[384,256]{1,0:T(8,128)(2,1)} %get-tuple-element.7, bf16[384,256]{1,0:T(8,128)(2,1)} %get-tuple-element.8, bf16[384,256]{1,0:T(8,128)(2,1)} %get-tuple-element.9), kind=kOutput, calls=%fused_computation.14 | convolution fusion | flops 1413120000 | bytes 5832704 | tf_op jit(solution)/shard_map/dot_general | solution.py:65
  249.5 26.1 %all-to-all-done.6 = bf16[8,48,1792]{2,1,0:T(8,128)(2,1)S(1)} async-done(((bf16[8,48,1792]{2,1,0:T(8,128)(2,1)}), bf16[8,48,1792]{2,1,0:T(8,128)(2,1)S(1)}, u32[]{:S(2)}, u32[]{:S(2)}) %all-to-all-start.6) | async-done | bytes 1376288 | tf_op jit(solution)/shard_map/all_to_all | solution.py:19
  275.6 5.4 %all-to-all-start.7 = ((bf16[8,48,1792]{2,1,0:T(8,128)(2,1)}), bf16[8,48,1792]{2,1,0:T(8,128)(2,1)}, u32[]{:S(2)}, u32[]{:S(2)}) async-start(bf16[8,48,1792]{2,1,0:T(8,128)(2,1)} %bitcast.139), calls=%async_computation.7 | async-start | bytes 2752512 | tf_op jit(solution)/shard_map/all_to_all | solution.py:19
  281.0 0.4 convert_element_type.75
  281.4 0.3 copy-done.9
  281.7 0.7 copy.13
  282.4 0.2 copy.15
  282.6 0.9 copy-done.1
  283.5 1.4 fusion.3
  284.9 3.1 collective-permute-start
  287.9 24.3 %all-to-all-done.7 = bf16[8,48,1792]{2,1,0:T(8,128)(2,1)} async-done(((bf16[8,48,1792]{2,1,0:T(8,128)(2,1)}), bf16[8,48,1792]{2,1,0:T(8,128)(2,1)}, u32[]{:S(2)}, u32[]{:S(2)}) %all-to-all-start.7) | async-done | bytes 1376288 | tf_op jit(solution)/shard_map/all_to_all | solution.py:19
  312.2 2.2 copy.14
  314.4 0.2 copy.16
  314.6 0.1 copy-done.2
  314.7 0.4 fusion.2
  315.1 1.6 collective-permute-start.1
  316.8 0.0 collective-permute-done
  316.8 10.3 %collective-permute-done.1 = bf16[64,7168]{1,0:T(8,128)(2,1)S(1)} collective-permute-done((bf16[64,7168]{1,0:T(8,128)(2,1)S(1)}, bf16[64,7168]{1,0:T(8,128)(2,1)S(1)}, u32[]{:S(2)}, u32[]{:S(2)}) %collective-permute-start.1) | collective-permute-done | bytes 917536 | tf_op jit(solution)/shard_map/ppermute | solution.py:15
  327.1 1.4 maximum_bitcast_fusion
  (16 shorter events, 0.0 us)
Async XLA Ops:
  0.0 5.4 %copy-start = (bf16[1,2,64,7168]{3,2,1,0:T(8,128)(2,1)S(1)}, bf16[1,2,64,7168]{3,2,1,0:T(8,128)(2,1)}, u32[]{:S(2)}) copy-start(bf16[1,2,64,7168]{3,2,1,0:T(8,128)(2,1)} %param.6) | copy-start | bytes 5505028
  5.9 1.2 copy-start.3
  48.0 46.2 %all-to-all-start.1 = ((bf16[4,1792,256]{2,1,0:T(8,128)(2,1)}), bf16[4,1792,256]{2,1,0:T(8,128)(2,1)}, u32[]{:S(2)}, u32[]{:S(2)}) async-start(bf16[4,1792,256]{2,1,0:T(8,128)(2,1)} %bitcast.136), calls=%async_computation.1 | async-start | bytes 7340032 | tf_op jit(solution)/shard_map/all_to_all | solution.py:19
  59.7 40.3 %copy-start.4 = (bf16[8,48,1792]{2,1,0:T(8,128)(2,1)S(1)}, bf16[8,48,1792]{2,1,0:T(8,128)(2,1)}, u32[]{:S(2)}) copy-start(bf16[8,48,1792]{2,1,0:T(8,128)(2,1)} %all_to_all.40) | copy-start | bytes 4128772
  94.3 36.9 %all-to-all-start = ((bf16[8,48,1792]{2,1,0:T(8,128)(2,1)}), bf16[8,48,1792]{2,1,0:T(8,128)(2,1)}, u32[]{:S(2)}, u32[]{:S(2)}) async-start(bf16[8,48,1792]{2,1,0:T(8,128)(2,1)} %bitcast.8), calls=%async_computation | async-start | bytes 2752512 | tf_op jit(solution)/shard_map/all_to_all | solution.py:19
  137.6 2.2 copy-start.6
  137.6 2.2 copy-start.7
  137.6 2.2 copy-start.8
  141.1 21.8 %all-to-all-start.3 = ((bf16[4,768,256]{2,1,0:T(8,128)(2,1)}), bf16[4,768,256]{2,1,0:T(8,128)(2,1)S(1)}, u32[]{:S(2)}, u32[]{:S(2)}) async-start(bf16[4,768,256]{2,1,0:T(8,128)(2,1)} %maximum_maximum_fusion), calls=%async_computation.3 | async-start | bytes 3145728 | tf_op jit(solution)/shard_map/all_to_all | solution.py:19
  163.0 46.1 %all-to-all-start.5 = ((bf16[4,256,1792]{1,2,0:T(8,128)(2,1)}), bf16[4,256,1792]{1,2,0:T(8,128)(2,1)}, u32[]{:S(2)}, u32[]{:S(2)}) async-start(bf16[4,256,1792]{1,2,0:T(8,128)(2,1)} %bitcast.129), calls=%async_computation.5 | async-start | bytes 7340032 | tf_op jit(solution)/shard_map/all_to_all | solution.py:19
  210.3 22.7 %all-to-all-start.4 = ((bf16[4,768,256]{2,1,0:T(8,128)(2,1)}), bf16[4,768,256]{2,1,0:T(8,128)(2,1)S(1)}, u32[]{:S(2)}, u32[]{:S(2)}) async-start(bf16[4,768,256]{2,1,0:T(8,128)(2,1)} %broadcast_in_dim.4), calls=%async_computation.4 | async-start | bytes 3145728 | tf_op jit(solution)/shard_map/all_to_all | solution.py:19
  238.6 5.8 %copy-start.5 = (bf16[384,256]{1,0:T(8,128)(2,1)S(1)}, bf16[384,256]{1,0:T(8,128)(2,1)}, u32[]{:S(2)}) copy-start(bf16[384,256]{1,0:T(8,128)(2,1)} %get-tuple-element.6) | copy-start | bytes 589828
  238.6 37.0 %all-to-all-start.6 = ((bf16[8,48,1792]{2,1,0:T(8,128)(2,1)}), bf16[8,48,1792]{2,1,0:T(8,128)(2,1)S(1)}, u32[]{:S(2)}, u32[]{:S(2)}) async-start(bf16[8,48,1792]{2,1,0:T(8,128)(2,1)} %bitcast.144), calls=%async_computation.6 | async-start | bytes 2752512 | tf_op jit(solution)/shard_map/all_to_all | solution.py:19
  275.6 36.7 %all-to-all-start.7 = ((bf16[8,48,1792]{2,1,0:T(8,128)(2,1)}), bf16[8,48,1792]{2,1,0:T(8,128)(2,1)}, u32[]{:S(2)}, u32[]{:S(2)}) async-start(bf16[8,48,1792]{2,1,0:T(8,128)(2,1)} %bitcast.139), calls=%async_computation.7 | async-start | bytes 2752512 | tf_op jit(solution)/shard_map/all_to_all | solution.py:19
  281.0 0.7 copy-start.9
  281.7 1.8 copy-start.1
  284.9 31.9 %collective-permute-start = (bf16[64,7168]{1,0:T(8,128)(2,1)}, bf16[64,7168]{1,0:T(8,128)(2,1)S(1)}, u32[]{:S(2)}, u32[]{:S(2)}) collective-permute-start(bf16[64,7168]{1,0:T(8,128)(2,1)} %fusion.3), channel_id=1, source_target_pairs={{0,8},{8,16},{16,24},{24,0},{1,9},{9,17},{17,25},{25,1},{2,10},{10... | collective-permute-start | bytes 2752520 | tf_op jit(solution)/shard_map/ppermute | solution.py:15
  312.2 2.5 copy-start.2
  315.1 12.0 %collective-permute-start.1 = (bf16[64,7168]{1,0:T(8,128)(2,1)S(1)}, bf16[64,7168]{1,0:T(8,128)(2,1)S(1)}, u32[]{:S(2)}, u32[]{:S(2)}) collective-permute-start(bf16[64,7168]{1,0:T(8,128)(2,1)S(1)} %fusion.2), channel_id=1, source_target_pairs={{0,8},{8,16},{16,24},{24,0},{1,9},{9,17},{17,25},{25,1},{2,10},{10... | collective-permute-start | bytes 2752520 | tf_op jit(solution)/shard_map/ppermute | solution.py:15

commit v3 on v1

v3 whole, which is shorter than its diff:
```python
import functools

import jax
import jax.numpy as jnp
from jax import lax
from jax.experimental import pallas as pl
from jax.experimental.pallas import tpu as pltpu
from jax.sharding import PartitionSpec as P

LEVELS = 2


EPSILON = 1e-06
GROUP = 2**LEVELS
MESH = pl.DeviceIdType.MESH
F32, BF16 = jnp.float32, jnp.bfloat16


def remote(source, target, send, recv, **where):
    return pltpu.make_async_remote_copy(
        src_ref=source, dst_ref=target, send_sem=send, recv_sem=recv, device_id=where, device_id_type=MESH
    )


def each(low, high, body):
    def step(index, carry):
        body(index)
        return carry

    lax.fori_loop(low, high, step, 0)


def spread(
    n, pipes, place, act, gain, gate, up, down, up_out, down_out, arrived, act_out, place_out, gate_out,
    packed, wsend, wrecv, dsend, drecv, psend, precv, own,
):
    me, pipe = lax.axis_index("expert"), lax.axis_index("pipe")
    first = (me // GROUP) * GROUP
    g = me - first
    part = packed.shape[-1]
    batches, experts = place.shape[:2]

    barrier = pltpu.get_barrier_semaphore()

    def greet(k):
        pl.semaphore_signal(barrier, inc=1, device_id={"expert": (me + k) % n}, device_id_type=MESH)

    each(1, n, greet)
    pl.semaphore_signal(barrier, inc=1, device_id={"pipe": (pipe + pipes - 1) % pipes}, device_id_type=MESH)
    pl.semaphore_wait(barrier, n)

    def columns(j):
        return pl.ds(pl.multiple_of(j * part, 128), part)

    waits = []
    for k in range(1, GROUP):
        j = (g + k) % GROUP
        copy = remote(up.at[j], up_out.at[g], wsend.at[0, k], wrecv.at[0, k], expert=first + j)
        copy.start()
        waits.append(copy)
    for i, (source, target) in enumerate(((act, act_out), (place, place_out), (gate, gate_out))):
        copy = remote(source, target, psend.at[i], precv.at[i], pipe=(pipe + 1) % pipes)
        copy.start()
        waits.append(copy)
    locals_ = [
        pltpu.make_async_copy(up.at[g], up_out.at[g], own.at[0]),
        pltpu.make_async_copy(down.at[:, columns(g)], down_out.at[g], own.at[1]),
    ]
    for copy in locals_:
        copy.start()

    for m in range(batches):
        wide = act[m].astype(F32)
        scale = lax.rsqrt(jnp.mean(wide * wide, axis=-1, keepdims=True) + EPSILON)
        normed = (wide * scale * gain[...].astype(F32)).astype(BF16)
        for e in range(experts):
            for j in range(GROUP):
                packed[m, e * GROUP + j] = jnp.dot(
                    place[m, e], normed[:, j * part : (j + 1) * part], preferred_element_type=F32
                ).astype(BF16)

        def send(k, m=m):
            d = (me + k) % n
            remote(packed.at[m, d], arrived.at[m, me], dsend.at[m, k], drecv.at[m, k], expert=d).start()

        each(1, n, send)
        copy = pltpu.make_async_copy(packed.at[m, me], arrived.at[m, me], own.at[2 + m])
        copy.start()
        locals_.append(copy)

    for k in range(1, GROUP):
        j = (g + k) % GROUP
        copy = remote(
            down.at[:, columns(j)], down_out.at[g], wsend.at[1, k], wrecv.at[1, k], expert=first + j
        )
        copy.start()
        waits.append(copy)

    for copy in locals_:
        copy.wait()
    for copy in waits:
        copy.wait()
    for m in range(batches):

        def finish(k, m=m):
            d = (me + k) % n
            remote(packed.at[m, d], arrived.at[m, me], dsend.at[m, k], drecv.at[m, k], expert=d).wait()

        each(1, n, finish)


def experts_kernel(
    n, pipes, x, up, down, ret, pres, sums, own_pre, hidden, out, ssend, srecv, hsend, hrecv, rsend, rrecv,
):
    me, pipe = lax.axis_index("expert"), lax.axis_index("pipe")
    group_index = me // GROUP
    first = group_index * GROUP
    g = me - first
    batches, capacity = ret.shape[0], ret.shape[2]
    units = up.shape[2]
    ahead, behind = (pipe + 1) % pipes, (pipe + pipes - 1) % pipes

    barrier = pltpu.get_barrier_semaphore()
    for k in range(1, GROUP):
        pl.semaphore_signal(
            barrier, inc=1, device_id={"expert": first + (g + k) % GROUP}, device_id_type=MESH
        )

    def greet(k):
        pl.semaphore_signal(barrier, inc=1, device_id={"pipe": behind, "expert": k}, device_id_type=MESH)

    each(0, n, greet)
    pl.semaphore_wait(barrier, n + GROUP - 1)

    copies = []
    for k in range(1, GROUP):
        j = (g + k) % GROUP
        pres[k] = jnp.dot(x[...], up[j], preferred_element_type=F32).astype(BF16)
        copy = remote(pres.at[k], sums.at[k], ssend.at[k], srecv.at[k], expert=first + j)
        copy.start()
        copies.append(copy)
    own_pre[...] = jnp.dot(x[...], up[g], preferred_element_type=F32)
    for copy in copies:
        copy.wait()
    total = own_pre[...]
    for k in range(1, GROUP):
        total = total + sums[k].astype(F32)
    mine = pl.ds(pl.multiple_of(g * units, 128), units)
    hidden[:, mine] = jax.nn.silu(total).astype(BF16)
    copies = []
    for k in range(1, GROUP):
        copy = remote(
            hidden.at[:, mine], hidden.at[:, mine], hsend.at[k], hrecv.at[k], expert=first + (g + k) % GROUP
        )
        copy.start()
        copies.append(copy)
    for copy in copies:
        copy.wait()

    blocks = n // GROUP
    tall = GROUP * capacity

    def block(index):
        m = index // blocks
        owner = (group_index + 1 + index) % blocks
        rows = pl.ds(pl.multiple_of((m * blocks + owner) * tall, 16), tall)
        out[rows, :] = jnp.dot(hidden[rows, :], down[...], preferred_element_type=F32).astype(BF16)
        for j in range(GROUP):
            target = owner * GROUP + j
            give(m, target).start()

    def give(m, target):
        rows = pl.ds(pl.multiple_of((m * n + target) * capacity, 16), capacity)
        return remote(
            out.at[rows, :], ret.at[m, me], rsend.at[m, target], rrecv.at[m, me], pipe=ahead, expert=target
        )

    each(0, batches * blocks, block)

    def finish(index):
        m, source = index // n, index % n
        give(m, source).wait_send()
        rows = pl.ds(pl.multiple_of(index * capacity, 16), capacity)
        remote(
            out.at[rows, :], ret.at[m, source], rsend.at[m, source], rrecv.at[m, source],
            pipe=ahead, expert=source,
        ).wait_recv()

    each(0, batches * n, finish)


def local(pipes, activations, expert_ids, gate_values, norm_gain, up_weight, down_weight):
    n = lax.axis_size("expert")
    experts = n // GROUP
    _, batches, tok, width = activations.shape
    part = width // GROUP
    units = up_weight.shape[2]
    capacity = max(2, 3 * tok // (2 * experts))
    capacity = (capacity + 15) // 16 * 16
    rows = batches * n * capacity

    onehot = (expert_ids[0][..., None] == jnp.arange(experts, dtype=jnp.int32)).astype(jnp.int32)
    ranking = jnp.sum((jnp.cumsum(onehot, axis=1) - onehot) * onehot, axis=-1)
    slot = expert_ids[0] * capacity + ranking
    slots = jnp.arange(experts * capacity, dtype=jnp.int32).reshape(1, experts, capacity, 1)
    place = (slot[:, None, None, :] == slots).astype(BF16)

    vmem, far = pl.BlockSpec(memory_space=pltpu.VMEM), pl.BlockSpec(memory_space=pl.ANY)
    shape, sem = jax.ShapeDtypeStruct, pltpu.SemaphoreType.DMA
    up_part, down_part, arrived, act_prev, place_prev, gate_prev = pl.pallas_call(
        functools.partial(spread, n, pipes),
        out_shape=(
            shape((GROUP, part, units), BF16),
            shape((GROUP, units, part), BF16),
            shape((batches, n, capacity, part), BF16),
            shape((batches, tok, width), BF16),
            shape(place.shape, BF16),
            shape((batches, tok), F32),
        ),
        in_specs=[vmem] * 4 + [far] * 2,
        out_specs=(far,) * 6,
        scratch_shapes=[
            pltpu.VMEM((batches, n, capacity, part), BF16),
            sem((2, GROUP)),
            sem((2, GROUP)),
            sem((batches, n)),
            sem((batches, n)),
            sem((3,)),
            sem((3,)),
            sem((2 + batches,)),
        ],
        compiler_params=pltpu.CompilerParams(
            collective_id=0, has_side_effects=True, vmem_limit_bytes=40 * 2**20
        ),
    )(
        place,
        activations[0],
        norm_gain,
        gate_values[0],
        up_weight[0].reshape(GROUP, part, units),
        down_weight[0],
    )

    returned = pl.pallas_call(
        functools.partial(experts_kernel, n, pipes),
        out_shape=shape((batches, n, capacity, part), BF16),
        in_specs=[vmem] * 3,
        out_specs=far,
        scratch_shapes=[
            pltpu.VMEM((GROUP, rows, units), BF16),
            pltpu.VMEM((GROUP, rows, units), BF16),
            pltpu.VMEM((rows, units), F32),
            pltpu.VMEM((rows, GROUP * units), BF16),
            pltpu.VMEM((rows, part), BF16),
            sem((GROUP,)),
            sem((GROUP,)),
            sem((GROUP,)),
            sem((GROUP,)),
            sem((batches, n)),
            sem((batches, n)),
        ],
        compiler_params=pltpu.CompilerParams(
            collective_id=1, has_side_effects=True, vmem_limit_bytes=60 * 2**20
        ),
    )(arrived.reshape(rows, part), up_part, down_part.reshape(GROUP * units, part))

    returned = returned.reshape(batches, experts, GROUP, capacity, part)
    finished = []
    for m in range(batches):
        table = returned[m].transpose(0, 2, 1, 3).reshape(experts * capacity, width)
        expert_out = lax.dot_general(
            place_prev[m].reshape(experts * capacity, tok),
            table,
            (((0,), (0,)), ((), ())),
            preferred_element_type=F32,
        )
        finished.append((act_prev[m].astype(F32) + gate_prev[m][:, None] * expert_out).astype(BF16))
    return jnp.stack(finished)[None]


def solution(mesh):
    placed = (
        P("pipe", None, "expert", None),
        P("pipe", None, "expert"),
        P("pipe", None, "expert"),
        P("pipe", None),
        P("pipe", None, "expert"),
        P("pipe", "expert", None),
    )
    return jax.shard_map(
        functools.partial(local, mesh.shape["pipe"]),
        mesh=mesh,
        in_specs=placed,
        out_specs=P("pipe", None, "expert", None),
        check_vma=False,
    )
```

time: 543 us -> 262 us (0.48)
  waiting for transfers between devices: 474 us -> 0 us
  Pallas kernels: 0 us -> 245 us
  matrix products: 31.9 us -> 0.95 us
  between operations: 13.9 us -> 0.11 us
  local copies, waits for them, and re-layouts: 1.52 us -> 11.8 us
  other arithmetic: 9.52 us -> 3.88 us
  blocking collectives: 5.61 us -> 0 us
    reduce_scatter x2 -> x0, waiting for transfers between devices: 254 us -> none  [one_batch(): lax.psum_scatter(partial_value, 'expert', scatter_dimension=0, tiled=True)]
    pallas_call x0 -> x2, Pallas kernels: none -> 245 us  [the longest x1 133 us: local(): pl.pallas_call(functools.partial(spread, n, pipes), out_shape=(shape((GRO...]
    all_gather x2 -> x0, waiting for transfers between devices: 199 us -> none  [one_batch(): every = lax.all_gather(normed, 'expert', axis=0, tiled=True)]
    dot_general x2, matrix products: 31.9 us -> 0.95 us  [local(): lax.dot_general(place_prev[m].reshape(experts * capacity, tok), table, ((...]
    ppermute x2 -> x0, waiting for transfers between devices: 20.1 us -> none  [from_behind(): return lax.ppermute(value, axis, pairs)]
    unnamed x13 -> x14, local copies, waits for them, and re-layouts: 1.52 us -> 8.43 us
    unnamed x1 -> x0, blocking collectives: 5.61 us -> none
  transfers between devices with their start and end apart: 6 -> 0, of which waited for: 6 -> 0; matrix products, arithmetic and copies ran while one was open for 6% -> 0% of each run, Pallas kernels for 0% -> 0%
where the time goes in v3:
time: 262 us
  Pallas kernels  245 us (94%)
  local copies, waits for them, and re-layouts  11.8 us (5%)
  other arithmetic  3.88 us (1%)
    pallas_call x1, Pallas kernels, local(): pl.pallas_call(functools.partial(spread, n, pipes), out_shape=(shape((GRO...  133 us
    pallas_call x1, Pallas kernels, local(): pl.pallas_call(functools.partial(experts_kernel, n, pipes), out_shape=sha...  112 us
    unnamed x14, local copies, waits for them, and re-layouts  8.43 us

profile of v3, /device:TPU:29, one launch (start us, length us, event | category | flops | bytes accessed | tf_op | source)
XLA Modules:
  0.0 262.2 jit_solution(18349796414764936126)
XLA Ops:
  0.0 0.8 fusion.6
  0.8 0.1 reduce_window_sum.11
  0.9 0.9 select_reduce_fusion
  1.7 0.7 multiply_add_fusion.1
  2.4 0.1 compare_convert_fusion.place
  2.5 0.0 copy-start.3
  2.5 1.5 copy-done.3
  4.0 0.0 copy-start.4
  4.0 0.7 copy-done.4
  4.8 0.0 copy-start.5
  4.8 0.7 copy-done.5
  5.4 133.3 %shard_map.64 = (bf16[4,1792,256]{2,1,0:T(8,128)(2,1)S(1)}, bf16[4,256,1792]{2,1,0:T(8,128)(2,1)S(1)}, bf16[2,8,48,1792]{3,2,1,0:T(8,128)(2,1)S(1)}, bf16[2,64,7...) custom-call(bf16[2,2,48,64]{3,2,1,0:T(8,128)(2,1)S(1)} %compare_convert_fusion.place, ...), custom_call_target="tpu_custom_call" | custom-call | tf_op jit(solution)/shard_map/pallas_call | solution.py:210
  138.7 0.0 copy-start
  138.7 1.8 copy-done
  140.5 0.0 copy-start.1
  140.5 1.8 copy-done.1
  142.4 0.0 copy-start.2
  142.4 1.6 copy-done.2
  143.9 112.2 %shard_map.65 = bf16[2,8,48,1792]{3,2,1,0:T(8,128)(2,1)} custom-call(bf16[768,1792]{1,0:T(8,128)(2,1)} %bitcast.41, bf16[4,1792,256]{2,1,0:T(8,128)(2,1)} %copy-done, bf16[1024,1792]{1,0:T(8,128)(2,1)} %bitcast.40), custom_call_target="tpu_custom_call" | custom-call | tf_op jit(solution)/shard_map/pallas_call | solution.py:244
  256.1 1.9 fusion.7
  258.0 0.7 copy.7
  258.7 0.2 copy.9
  258.9 0.5 fusion.4
  259.4 0.7 copy.8
  260.1 0.2 copy.10
  260.3 0.5 fusion.5
  260.8 1.4 maximum_bitcast_fusion
  (3 shorter events, 0.0 us)
Async XLA Ops:
  2.5 1.5 copy-start.3
  4.0 0.7 copy-start.4
  4.8 0.7 copy-start.5
  138.7 1.8 copy-start
  140.5 1.8 copy-start.1
  142.4 1.6 copy-start.2

commit v4 on v1

v4 whole, which is shorter than its diff:
```python
import functools

import jax
import jax.numpy as jnp
from jax import lax
from jax.experimental import pallas as pl
from jax.experimental.pallas import tpu as pltpu
from jax.sharding import PartitionSpec as P

LEVELS = 2


EPSILON = 1e-06
GROUP = 2**LEVELS
MESH = pl.DeviceIdType.MESH
F32, BF16 = jnp.float32, jnp.bfloat16


def remote(source, target, send, recv, **where):
    return pltpu.make_async_remote_copy(
        src_ref=source, dst_ref=target, send_sem=send, recv_sem=recv, device_id=where, device_id_type=MESH
    )


def each(low, high, body):
    def step(index, carry):
        body(index)
        return carry

    lax.fori_loop(low, high, step, 0)


def layer_kernel(
    n, pipes, place, act, gain, gate, up, down, ret, act_out, place_out, gate_out,
    packed, x, up_all, down_all, pres, sums, own_pre, hidden, out,
    usend, urecv, dsend, drecv, psend, precv, xsend, xrecv, ssend, srecv, hsend, hrecv, rsend, rrecv, own,
):
    me, pipe = lax.axis_index("expert"), lax.axis_index("pipe")
    group_index = me // GROUP
    first = group_index * GROUP
    g = me - first
    batches, experts, capacity = place.shape[:3]
    part, units = up.shape[1:]
    ahead, behind = (pipe + 1) % pipes, (pipe + pipes - 1) % pipes
    blocks = n // GROUP
    tall = GROUP * capacity

    barrier = pltpu.get_barrier_semaphore()

    def greet(k):
        pl.semaphore_signal(barrier, inc=1, device_id={"expert": (me + k) % n}, device_id_type=MESH)

    def greet_behind(k):
        pl.semaphore_signal(barrier, inc=1, device_id={"pipe": behind, "expert": k}, device_id_type=MESH)

    each(1, n, greet)
    each(0, n, greet_behind)
    pl.semaphore_wait(barrier, 2 * n - 1)

    def columns(j):
        return pl.ds(pl.multiple_of(j * part, 128), part)

    def share(j):
        return pl.ds(pl.multiple_of(j * units, 128), units)

    def rows_of(d):
        return pl.ds(pl.multiple_of(d * capacity, 16), capacity)

    peers = [(k, (g + k) % GROUP) for k in range(1, GROUP)]
    ups = [remote(up.at[j], up_all.at[g], usend.at[k], urecv.at[k], expert=first + j) for k, j in peers]
    downs = [
        remote(
            down.at[:, columns(j)], down_all.at[share(g), :], dsend.at[k], drecv.at[k], expert=first + j
        )
        for k, j in peers
    ]
    shifts = [
        remote(source, target, psend.at[i], precv.at[i], pipe=ahead)
        for i, (source, target) in enumerate(((act, act_out), (place, place_out), (gate, gate_out)))
    ]

    def dispatch(m, k):
        d = (me + k) % n
        return remote(packed.at[m, d], x.at[m, rows_of(me), :], xsend.at[m, k], xrecv.at[m, k], expert=d)

    for copy in ups:
        copy.start()
    own_up = pltpu.make_async_copy(up.at[g], up_all.at[g], own.at[0])
    own_down = pltpu.make_async_copy(down.at[:, columns(g)], down_all.at[share(g), :], own.at[1])
    own_up.start()
    own_down.start()
    own_rows = []
    for m in range(batches):
        wide = act[m].astype(F32)
        scale = lax.rsqrt(jnp.mean(wide * wide, axis=-1, keepdims=True) + EPSILON)
        normed = (wide * scale * gain[...].astype(F32)).astype(BF16)
        for e in range(experts):
            for j in range(GROUP):
                packed[m, e * GROUP + j] = jnp.dot(
                    place[m, e], normed[:, j * part : (j + 1) * part], preferred_element_type=F32
                ).astype(BF16)
        each(1, n, lambda k, m=m: dispatch(m, k).start())
        copy = pltpu.make_async_copy(packed.at[m, me], x.at[m, rows_of(me), :], own.at[2 + m])
        copy.start()
        own_rows.append(copy)
    for copy in shifts:
        copy.start()

    def summing(m, k, j):
        return remote(pres.at[m, k], sums.at[m, k], ssend.at[m, k], srecv.at[m, k], expert=first + j)

    def sharing(m, k, j):
        mine = hidden.at[m, :, share(g)]
        return remote(mine, mine, hsend.at[m, k], hrecv.at[m, k], expert=first + j)

    own_up.wait()
    for copy in ups:
        copy.wait_recv()
    for m in range(batches):
        own_rows[m].wait()
        each(1, n, lambda k, m=m: dispatch(m, k).wait_recv())
        for k, j in peers:
            pres[m, k] = jnp.dot(x[m], up_all[j], preferred_element_type=F32).astype(BF16)
            summing(m, k, j).start()
        if m == 0:
            for copy in downs:
                copy.start()
        own_pre[...] = jnp.dot(x[m], up_all[g], preferred_element_type=F32)
        for k, j in peers:
            summing(m, k, j).wait_recv()
        total = own_pre[...]
        for k in range(1, GROUP):
            total = total + sums[m, k].astype(F32)
        hidden[m, :, share(g)] = jax.nn.silu(total).astype(BF16)
        for k, j in peers:
            sharing(m, k, j).start()

    def give(m, target):
        return remote(
            out.at[m, rows_of(target), :], ret.at[m, me], rsend.at[m, target], rrecv.at[m, me],
            pipe=ahead, expert=target,
        )

    own_down.wait()
    for copy in downs:
        copy.wait_recv()
    for m in range(batches):
        for k, j in peers:
            sharing(m, k, j).wait_recv()

        def block(index, m=m):
            owner = (group_index + 1 + index) % blocks
            rows = pl.ds(pl.multiple_of(owner * tall, 16), tall)
            out[m, rows, :] = jnp.dot(
                hidden[m, rows, :], down_all[...], preferred_element_type=F32
            ).astype(BF16)
            for j in range(GROUP):
                give(m, owner * GROUP + j).start()

        each(0, blocks, block)

    for copy in ups + downs:
        copy.wait_send()
    for copy in shifts:
        copy.wait()
    for m in range(batches):
        each(1, n, lambda k, m=m: dispatch(m, k).wait_send())
        for k, j in peers:
            summing(m, k, j).wait_send()
            sharing(m, k, j).wait_send()

        def finish(source, m=m):
            give(m, source).wait_send()
            remote(
                out.at[m, rows_of(source), :], ret.at[m, source], rsend.at[m, source],
                rrecv.at[m, source], pipe=ahead, expert=source,
            ).wait_recv()

        each(0, n, finish)


def local(pipes, activations, expert_ids, gate_values, norm_gain, up_weight, down_weight):
    n = lax.axis_size("expert")
    experts = n // GROUP
    _, batches, tok, width = activations.shape
    part = width // GROUP
    units = up_weight.shape[2]
    capacity = max(2, 3 * tok // (2 * experts))
    capacity = (capacity + 15) // 16 * 16
    rows = n * capacity

    onehot = (expert_ids[0][..., None] == jnp.arange(experts, dtype=jnp.int32)).astype(jnp.int32)
    ranking = jnp.sum((jnp.cumsum(onehot, axis=1) - onehot) * onehot, axis=-1)
    slot = expert_ids[0] * capacity + ranking
    slots = jnp.arange(experts * capacity, dtype=jnp.int32).reshape(1, experts, capacity, 1)
    place = (slot[:, None, None, :] == slots).astype(BF16)

    vmem, far = pl.BlockSpec(memory_space=pltpu.VMEM), pl.BlockSpec(memory_space=pl.ANY)
    shape, sem = jax.ShapeDtypeStruct, pltpu.SemaphoreType.DMA
    returned, act_prev, place_prev, gate_prev = pl.pallas_call(
        functools.partial(layer_kernel, n, pipes),
        out_shape=(
            shape((batches, n, capacity, part), BF16),
            shape((batches, tok, width), BF16),
            shape(place.shape, BF16),
            shape((batches, tok), F32),
        ),
        in_specs=[vmem] * 4 + [far] * 2,
        out_specs=(far,) * 4,
        scratch_shapes=[
            pltpu.VMEM((batches, n, capacity, part), BF16),
            pltpu.VMEM((batches, rows, part), BF16),
            pltpu.VMEM((GROUP, part, units), BF16),
            pltpu.VMEM((GROUP * units, part), BF16),
            pltpu.VMEM((batches, GROUP, rows, units), BF16),
            pltpu.VMEM((batches, GROUP, rows, units), BF16),
            pltpu.VMEM((rows, units), F32),
            pltpu.VMEM((batches, rows, GROUP * units), BF16),
            pltpu.VMEM((batches, rows, part), BF16),
            sem((GROUP,)),
            sem((GROUP,)),
            sem((GROUP,)),
            sem((GROUP,)),
            sem((3,)),
            sem((3,)),
            sem((batches, n)),
            sem((batches, n)),
            sem((batches, GROUP)),
            sem((batches, GROUP)),
            sem((batches, GROUP)),
            sem((batches, GROUP)),
            sem((batches, n)),
            sem((batches, n)),
            sem((2 + batches,)),
        ],
        compiler_params=pltpu.CompilerParams(
            collective_id=0, has_side_effects=True, vmem_limit_bytes=60 * 2**20
        ),
    )(
        place,
        activations[0],
        norm_gain,
        gate_values[0],
        up_weight[0].reshape(GROUP, part, units),
        down_weight[0],
    )

    returned = returned.reshape(batches, experts, GROUP, capacity, part)
    finished = []
    for m in range(batches):
        table = returned[m].transpose(0, 2, 1, 3).reshape(experts * capacity, width)
        expert_out = lax.dot_general(
            place_prev[m].reshape(experts * capacity, tok),
            table,
            (((0,), (0,)), ((), ())),
            preferred_element_type=F32,
        )
        finished.append((act_prev[m].astype(F32) + gate_prev[m][:, None] * expert_out).astype(BF16))
    return jnp.stack(finished)[None]


def solution(mesh):
    placed = (
        P("pipe", None, "expert", None),
        P("pipe", None, "expert"),
        P("pipe", None, "expert"),
        P("pipe", None),
        P("pipe", None, "expert"),
        P("pipe", "expert", None),
    )
    return jax.shard_map(
        functools.partial(local, mesh.shape["pipe"]),
        mesh=mesh,
        in_specs=placed,
        out_specs=P("pipe", None, "expert", None),
        check_vma=False,
    )
```

time: 543 us -> 239 us (0.44)
  waiting for transfers between devices: 474 us -> 0 us
  Pallas kernels: 0 us -> 226 us
  matrix products: 31.9 us -> 0.93 us
  between operations: 13.9 us -> 0.08 us
  blocking collectives: 5.61 us -> 0 us
    reduce_scatter x2 -> x0, waiting for transfers between devices: 254 us -> none  [one_batch(): lax.psum_scatter(partial_value, 'expert', scatter_dimension=0, tiled=True)]
    pallas_call x0 -> x1, Pallas kernels: none -> 226 us  [local(): pl.pallas_call(functools.partial(layer_kernel, n, pipes), out_shape=(shap...]
    all_gather x2 -> x0, waiting for transfers between devices: 199 us -> none  [one_batch(): every = lax.all_gather(normed, 'expert', axis=0, tiled=True)]
    dot_general x2, matrix products: 31.9 us -> 0.93 us  [local(): lax.dot_general(place_prev[m].reshape(experts * capacity, tok), table, ((...]
    ppermute x2 -> x0, waiting for transfers between devices: 20.1 us -> none  [from_behind(): return lax.ppermute(value, axis, pairs)]
    unnamed x1 -> x0, blocking collectives: 5.61 us -> none
  transfers between devices with their start and end apart: 6 -> 0, of which waited for: 6 -> 0; matrix products, arithmetic and copies ran while one was open for 6% -> 0% of each run, Pallas kernels for 0% -> 0%
where the time goes in v4:
time: 239 us; the launch traced here: 238 us
  Pallas kernels  226 us (95%)
  local copies, waits for them, and re-layouts  6.49 us (3%)
  other arithmetic  4.5 us (2%)
    pallas_call x1, Pallas kernels, local(): pl.pallas_call(functools.partial(layer_kernel, n, pipes), out_shape=(shap...  226 us

profile of v4, /device:TPU:29, one launch (start us, length us, event | category | flops | bytes accessed | tf_op | source)
XLA Modules:
  0.0 238.5 jit_solution(10410103868795526384)
XLA Ops:
  0.0 0.8 fusion.6
  0.8 0.1 reduce_window_sum.11
  0.9 0.9 select_reduce_fusion
  1.7 0.7 multiply_add_fusion.1
  2.4 0.7 compare_convert_fusion.place
  3.1 226.5 %shard_map.64 = (bf16[2,8,48,1792]{3,2,1,0:T(8,128)(2,1)}, bf16[2,64,7168]{2,1,0:T(8,128)(2,1)}, bf16[2,2,48,64]{3,2,1,0:T(8,128)(2,1)}, f32[2,64]{1,0:T(2,128)}) custom-call(bf16[2,2,48,64]{3,2,1,0:T(8,128)(2,1)} %compare_convert_fusion.place, bf16[2,64,7168]{2,1,0:T(8,128)(2,1)} %bitcast.46, bf16[1,7168]{1,0:T(2,128)(2,1)} %gain.1, f32[2,64]{1,0:T(2,128)} %bitcast.51, ...), custom_call_target="tpu_custom_call" | custom-call | tf_op jit(solution)/shard_map/pallas_call | solution.py:200
  229.6 0.7 slice_bitcast_fusion.1
  230.4 0.8 fusion.8
  231.1 1.9 fusion.7
  233.0 0.7 copy.7
  233.8 0.0 copy-start
  233.8 0.2 copy.9
  233.9 1.3 copy-done
  235.3 0.5 fusion.4
  235.7 0.7 copy.8
  236.4 0.2 copy.10
  236.6 0.5 fusion.5
  237.1 1.4 maximum_bitcast_fusion
  (1 shorter events, 0.0 us)
Async XLA Ops:
  233.8 1.5 copy-start

commit v5 on v4

--- a/solution.py
+++ b/solution.py
@@ -99,12 +99,11 @@
                 packed[m, e * GROUP + j] = jnp.dot(
                     place[m, e], normed[:, j * part : (j + 1) * part], preferred_element_type=F32
                 ).astype(BF16)
-        each(1, n, lambda k, m=m: dispatch(m, k).start())
+        if m == 0:
+            each(1, n, lambda k: dispatch(0, k).start())
         copy = pltpu.make_async_copy(packed.at[m, me], x.at[m, rows_of(me), :], own.at[2 + m])
         copy.start()
         own_rows.append(copy)
-    for copy in shifts:
-        copy.start()
 
     def summing(m, k, j):
         return remote(pres.at[m, k], sums.at[m, k], ssend.at[m, k], srecv.at[m, k], expert=first + j)
@@ -122,8 +121,10 @@
         for k, j in peers:
             pres[m, k] = jnp.dot(x[m], up_all[j], preferred_element_type=F32).astype(BF16)
             summing(m, k, j).start()
+        if m + 1 < batches:
+            each(1, n, lambda k, m=m: dispatch(m + 1, k).start())
         if m == 0:
-            for copy in downs:
+            for copy in downs + shifts:
                 copy.start()
         own_pre[...] = jnp.dot(x[m], up_all[g], preferred_element_type=F32)
         for k, j in peers:
@@ -135,9 +136,12 @@
         for k, j in peers:
             sharing(m, k, j).start()
 
+    def slots_of(m, source):
+        return ret.at[m, rows_of(source // GROUP), columns(source % GROUP)]
+
     def give(m, target):
         return remote(
-            out.at[m, rows_of(target), :], ret.at[m, me], rsend.at[m, target], rrecv.at[m, me],
+            out.at[m, rows_of(target), :], slots_of(m, me), rsend.at[m, target], rrecv.at[m, me],
             pipe=ahead, expert=target,
         )
 
@@ -172,7 +176,7 @@
         def finish(source, m=m):
             give(m, source).wait_send()
             remote(
-                out.at[m, rows_of(source), :], ret.at[m, source], rsend.at[m, source],
+                out.at[m, rows_of(source), :], slots_of(m, source), rsend.at[m, source],
                 rrecv.at[m, source], pipe=ahead, expert=source,
             ).wait_recv()
 
@@ -200,7 +204,7 @@
     returned, act_prev, place_prev, gate_prev = pl.pallas_call(
         functools.partial(layer_kernel, n, pipes),
         out_shape=(
-            shape((batches, n, capacity, part), BF16),
+            shape((batches, experts * capacity, width), BF16),
             shape((batches, tok, width), BF16),
             shape(place.shape, BF16),
             shape((batches, tok), F32),
@@ -245,13 +249,11 @@
         down_weight[0],
     )
 
-    returned = returned.reshape(batches, experts, GROUP, capacity, part)
     finished = []
     for m in range(batches):
-        table = returned[m].transpose(0, 2, 1, 3).reshape(experts * capacity, width)
         expert_out = lax.dot_general(
             place_prev[m].reshape(experts * capacity, tok),
-            table,
+            returned[m],
             (((0,), (0,)), ((), ())),
             preferred_element_type=F32,
         )

time: 239 us -> 238 us (level); the launches traced: 238 us -> 234 us
  local copies, waits for them, and re-layouts: 6.49 us -> 1.59 us
  matrix products: 0.93 us -> 3.7 us
    dot_general x2, matrix products: 0.93 us -> 3.7 us  [local(): lax.dot_general(place_prev[m].reshape(experts * capacity, tok), returned[...]
where the time goes in v5:
time: 238 us; the launch traced here: 234 us
  Pallas kernels  224 us (94%)
  other arithmetic  4.5 us (2%)
  matrix products  3.7 us (2%)
    pallas_call x1, Pallas kernels, local(): pl.pallas_call(functools.partial(layer_kernel, n, pipes), out_shape=(shap...  224 us

profile of v5, /device:TPU:29, one launch (start us, length us, event | category | flops | bytes accessed | tf_op | source)
XLA Modules:
  0.0 234.1 jit_solution(14543648841243228889)
XLA Ops:
  0.0 0.8 fusion.10
  0.8 0.1 reduce_window_sum.11
  0.9 0.9 select_reduce_fusion
  1.7 0.7 multiply_add_fusion.1
  2.4 0.7 compare_convert_fusion.place
  3.1 224.2 %shard_map.64 = (bf16[2,96,7168]{2,1,0:T(8,128)(2,1)}, bf16[2,64,7168]{2,1,0:T(8,128)(2,1)}, bf16[2,2,48,64]{3,2,1,0:T(8,128)(2,1)}, f32[2,64]{1,0:T(2,128)}) custom-call(bf16[2,2,48,64]{3,2,1,0:T(8,128)(2,1)} %compare_convert_fusion.place, bf16[2,64,7168]{2,1,0:T(8,128)(2,1)} %bitcast.34, bf16[1,7168]{1,0:T(2,128)(2,1)} %gain.1, f32[2,64]{1,0:T(2,128)} %bitcast.39, ...), custom_call_target="tpu_custom_call" | custom-call | tf_op jit(solution)/shard_map/pallas_call | solution.py:204
  227.4 0.0 copy-start
  227.4 0.8 slice_bitcast_fusion.1
  228.2 0.8 fusion.11
  229.0 2.0 fusion.5
  231.0 0.0 copy-done
  231.0 1.7 fusion.4
  232.7 1.4 maximum_bitcast_fusion
  (1 shorter events, 0.0 us)
Async XLA Ops:
  227.4 3.6 %copy-start = (bf16[2,96,7168]{2,1,0:T(8,128)(2,1)S(1)}, bf16[2,96,7168]{2,1,0:T(8,128)(2,1)}, u32[]{:S(2)}) copy-start(bf16[2,96,7168]{2,1,0:T(8,128)(2,1)} %get-tuple-element.12) | copy-start | bytes 8257540

commit v6 on v5

--- a/solution.py
+++ b/solution.py
@@ -112,6 +112,15 @@
         mine = hidden.at[m, :, share(g)]
         return remote(mine, mine, hsend.at[m, k], hrecv.at[m, k], expert=first + j)
 
+    def slots_of(m, source):
+        return ret.at[m, rows_of(source // GROUP), columns(source % GROUP)]
+
+    def give(m, target):
+        return remote(
+            out.at[m, rows_of(target), :], slots_of(m, me), rsend.at[m, target], rrecv.at[m, me],
+            pipe=ahead, expert=target,
+        )
+
     own_up.wait()
     for copy in ups:
         copy.wait_recv()
@@ -121,10 +130,8 @@
         for k, j in peers:
             pres[m, k] = jnp.dot(x[m], up_all[j], preferred_element_type=F32).astype(BF16)
             summing(m, k, j).start()
-        if m + 1 < batches:
-            each(1, n, lambda k, m=m: dispatch(m + 1, k).start())
         if m == 0:
-            for copy in downs + shifts:
+            for copy in downs:
                 copy.start()
         own_pre[...] = jnp.dot(x[m], up_all[g], preferred_element_type=F32)
         for k, j in peers:
@@ -135,20 +142,14 @@
         hidden[m, :, share(g)] = jax.nn.silu(total).astype(BF16)
         for k, j in peers:
             sharing(m, k, j).start()
-
-    def slots_of(m, source):
-        return ret.at[m, rows_of(source // GROUP), columns(source % GROUP)]
-
-    def give(m, target):
-        return remote(
-            out.at[m, rows_of(target), :], slots_of(m, me), rsend.at[m, target], rrecv.at[m, me],
-            pipe=ahead, expert=target,
-        )
-
-    own_down.wait()
-    for copy in downs:
-        copy.wait_recv()
-    for m in range(batches):
+        if m + 1 < batches:
+            each(1, n, lambda k, m=m: dispatch(m + 1, k).start())
+        if m == 0:
+            for copy in shifts:
+                copy.start()
+            own_down.wait()
+            for copy in downs:
+                copy.wait_recv()
         for k, j in peers:
             sharing(m, k, j).wait_recv()
 

time: 238 us -> 240 us (level)
  Pallas kernels: 224 us -> 227 us
    pallas_call x1, Pallas kernels: 224 us -> 227 us  [local(): pl.pallas_call(functools.partial(layer_kernel, n, pipes), out_shape=(shap...]
where the time goes in v6:
time: 240 us; the launch traced here: 237 us
  Pallas kernels  227 us (95%)
  other arithmetic  4.5 us (2%)
  matrix products  3.71 us (2%)
    pallas_call x1, Pallas kernels, local(): pl.pallas_call(functools.partial(layer_kernel, n, pipes), out_shape=(shap...  227 us

profile of v6, /device:TPU:29, one launch (start us, length us, event | category | flops | bytes accessed | tf_op | source)
XLA Modules:
  0.0 236.9 jit_solution(1209469556117262215)
XLA Ops:
  0.0 0.8 fusion.10
  0.8 0.1 reduce_window_sum.11
  0.9 0.9 select_reduce_fusion
  1.7 0.7 multiply_add_fusion.1
  2.4 0.7 compare_convert_fusion.place
  3.1 227.1 %shard_map.64 = (bf16[2,96,7168]{2,1,0:T(8,128)(2,1)}, bf16[2,64,7168]{2,1,0:T(8,128)(2,1)}, bf16[2,2,48,64]{3,2,1,0:T(8,128)(2,1)}, f32[2,64]{1,0:T(2,128)}) custom-call(bf16[2,2,48,64]{3,2,1,0:T(8,128)(2,1)} %compare_convert_fusion.place, bf16[2,64,7168]{2,1,0:T(8,128)(2,1)} %bitcast.34, bf16[1,7168]{1,0:T(2,128)(2,1)} %gain.1, f32[2,64]{1,0:T(2,128)} %bitcast.39, ...), custom_call_target="tpu_custom_call" | custom-call | tf_op jit(solution)/shard_map/pallas_call | solution.py:205
  230.2 0.0 copy-start
  230.2 0.8 slice_bitcast_fusion.1
  231.1 0.8 fusion.11
  231.8 2.1 fusion.5
  233.9 0.0 copy-done
  233.9 1.7 fusion.4
  235.6 1.4 maximum_bitcast_fusion
  (1 shorter events, 0.0 us)
Async XLA Ops:
  230.2 3.7 %copy-start = (bf16[2,96,7168]{2,1,0:T(8,128)(2,1)S(1)}, bf16[2,96,7168]{2,1,0:T(8,128)(2,1)}, u32[]{:S(2)}) copy-start(bf16[2,96,7168]{2,1,0:T(8,128)(2,1)} %get-tuple-element.12) | copy-start | bytes 8257540

commit v7 on v6

--- a/solution.py
+++ b/solution.py
@@ -101,6 +101,8 @@
                 ).astype(BF16)
         if m == 0:
             each(1, n, lambda k: dispatch(0, k).start())
+            for copy in downs:
+                copy.start()
         copy = pltpu.make_async_copy(packed.at[m, me], x.at[m, rows_of(me), :], own.at[2 + m])
         copy.start()
         own_rows.append(copy)
@@ -130,9 +132,8 @@
         for k, j in peers:
             pres[m, k] = jnp.dot(x[m], up_all[j], preferred_element_type=F32).astype(BF16)
             summing(m, k, j).start()
-        if m == 0:
-            for copy in downs:
-                copy.start()
+        if m + 1 < batches:
+            each(1, n, lambda k, m=m: dispatch(m + 1, k).start())
         own_pre[...] = jnp.dot(x[m], up_all[g], preferred_element_type=F32)
         for k, j in peers:
             summing(m, k, j).wait_recv()
@@ -142,8 +143,6 @@
         hidden[m, :, share(g)] = jax.nn.silu(total).astype(BF16)
         for k, j in peers:
             sharing(m, k, j).start()
-        if m + 1 < batches:
-            each(1, n, lambda k, m=m: dispatch(m + 1, k).start())
         if m == 0:
             for copy in shifts:
                 copy.start()

time: 240 us -> 245 us (1.021)
  Pallas kernels: 227 us -> 230 us
    pallas_call x1, Pallas kernels: 227 us -> 230 us  [local(): pl.pallas_call(functools.partial(layer_kernel, n, pipes), out_shape=(shap...]
where the time goes in v7:
time: 245 us; the launch traced here: 240 us
  Pallas kernels  230 us (94%)
  other arithmetic  4.5 us (2%)
  matrix products  3.72 us (2%)
    pallas_call x1, Pallas kernels, local(): pl.pallas_call(functools.partial(layer_kernel, n, pipes), out_shape=(shap...  230 us

profile of v7, /device:TPU:29, one launch (start us, length us, event | category | flops | bytes accessed | tf_op | source)
XLA Modules:
  0.0 240.2 jit_solution(17770729174515220762)
XLA Ops:
  0.0 0.8 fusion.10
  0.8 0.1 reduce_window_sum.11
  0.9 0.9 select_reduce_fusion
  1.7 0.7 multiply_add_fusion.1
  2.4 0.7 compare_convert_fusion.place
  3.1 230.4 %shard_map.64 = (bf16[2,96,7168]{2,1,0:T(8,128)(2,1)}, bf16[2,64,7168]{2,1,0:T(8,128)(2,1)}, bf16[2,2,48,64]{3,2,1,0:T(8,128)(2,1)}, f32[2,64]{1,0:T(2,128)}) custom-call(bf16[2,2,48,64]{3,2,1,0:T(8,128)(2,1)} %compare_convert_fusion.place, bf16[2,64,7168]{2,1,0:T(8,128)(2,1)} %bitcast.34, bf16[1,7168]{1,0:T(2,128)(2,1)} %gain.1, f32[2,64]{1,0:T(2,128)} %bitcast.39, ...), custom_call_target="tpu_custom_call" | custom-call | tf_op jit(solution)/shard_map/pallas_call | solution.py:204
  233.5 0.0 copy-start
  233.5 0.8 slice_bitcast_fusion.1
  234.3 0.8 fusion.11
  235.1 2.1 fusion.5
  237.2 0.0 copy-done
  237.2 1.7 fusion.4
  238.8 1.4 maximum_bitcast_fusion
  (1 shorter events, 0.0 us)
Async XLA Ops:
  233.5 3.7 %copy-start = (bf16[2,96,7168]{2,1,0:T(8,128)(2,1)S(1)}, bf16[2,96,7168]{2,1,0:T(8,128)(2,1)}, u32[]{:S(2)}) copy-start(bf16[2,96,7168]{2,1,0:T(8,128)(2,1)} %get-tuple-element.12) | copy-start | bytes 8257540
